TPU v7x, 32 devices: a whole 2x2x4 slice. The times are simulated.
32 devices in a mesh: groups: 2 (over y), servers: 4 (over z), heads: 4 (over x, core).
Axes of the slice: x: 2, y: 2, z: 4, core: 2. Of those that a mesh axis runs over, the one named last changes fastest.
Arguments:
- grad_out: bfloat16 [4096, 2048], P(('groups', 'servers')), parts along dimension 0, may hold values from -6 to 6
- out_weight: bfloat16 [2048, 4096], P(None, 'heads'), may hold values from -0.125 to 0.125
- queries: bfloat16 [4096, 4096], P(('groups', 'servers'), 'heads'), parts along dimension 0, may hold values from -2.5 to 2.5
- attn_out: bfloat16 [4096, 4096], P(('groups', 'servers'), 'heads'), parts along dimension 0, may hold values from -4 to 4
- lse: float32 [32, 4096], P('heads', ('groups', 'servers')), parts along dimension 1, may hold values from 5 to 6.5
- keys: bfloat16 [4096, 512], P(('groups', 'servers'), 'heads'), parts along dimension 0, may hold values from -2.5 to 2.5
- values: bfloat16 [4096, 512], P(('groups', 'servers'), 'heads'), parts along dimension 0, may hold values from -4 to 4
- prefix_keys: bfloat16 [256, 512], P(('groups', 'servers'), 'heads'), parts along dimension 0, may hold values from -2.5 to 2.5
- prefix_values: bfloat16 [256, 512], P(('groups', 'servers'), 'heads'), parts along dimension 0, may hold values from -4 to 4
- fork_owner: int32 [128, 1], P('groups'), parts along dimension 0, may hold values from 0 to 3; in each aligned block of 16 rows (0 to 15, 16 to 31, ...) at most 8 rows name the same one
- fork_root: int32 [128], P('groups'), parts along dimension 0, may hold values from 0 to 3
- fork_offset: int32 [128], P('groups'), parts along dimension 0, may hold values from 1 to 64
Outputs:
- grad_queries: bfloat16 [4096, 4096], P(('groups', 'servers'), 'heads'), parts along dimension 0
- grad_keys: bfloat16 [4096, 512], P(('groups', 'servers'), 'heads'), parts along dimension 0
- grad_values: bfloat16 [4096, 512], P(('groups', 'servers'), 'heads'), parts along dimension 0
- prefix_grad_keys: bfloat16 [256, 512], P(('groups', 'servers'), 'heads'), parts along dimension 0
- prefix_grad_values: bfloat16 [256, 512], P(('groups', 'servers'), 'heads'), parts along dimension 0
There are 2 independent parts, one for each index of `groups`. A program takes and returns all parts, laid end to end along the dimension named above; an argument that names none is the same for every part. Nothing has to cross between parts.
Inputs may be any that keep to these rules, and one draw needn't show every extreme that they name: `fork_owner`: row g names the owner of the rollout that continuation g forks from. Among the continuations of one owner (aligned blocks of 16 rows) no owner is named more than 8 times.
All inputs are finite; a program needn't handle non-finite values.
Results may differ from a plain program's by a relative error of at most 0.0061.
Values may be sent and summed in bfloat16 or wider, within the bound.
No kernel may reach another device: no remote copies, remote signals or barrier semaphores. Data moves between devices by JAX's collectives and lax.ppermute only.
A program may use at most 128 MiB of HBM per device.

v0:
```python
import math
import jax
import jax.numpy as jnp
from jax import lax
from jax.sharding import PartitionSpec as P

HD = 128
CH_DEV = 16
ROOTS_DEV = 4
RLEN = 64
CLEN = 16


def attend(query_heads, out_heads, lse_rows, delta_rows, key_heads, value_heads, mask_rows):
    tok_count, head_local, head_size = query_heads.shape
    key_count, shared_heads, _ = key_heads.shape
    group_size = head_local // shared_heads
    scaling = head_size ** (-0.5)
    block_rows = math.gcd(tok_count, 128)
    block_count = tok_count // block_rows
    contract = (((1,), (1,)), ((), ()))
    across = (((0,), (0,)), ((), ()))
    key_list = [key_heads[:, 0]]
    value_list = [value_heads[:, 0]]

    def block_step(totals, block_index):
        key_totals, value_totals = totals
        start = block_index * block_rows
        query_block = lax.dynamic_slice_in_dim(query_heads, start, block_rows, 0).reshape(
            block_rows, shared_heads, group_size, head_size
        )
        out_block = lax.dynamic_slice_in_dim(out_heads, start, block_rows, 0).reshape(
            block_rows, shared_heads, group_size, head_size
        )
        lse_block = lax.dynamic_slice_in_dim(lse_rows, start, block_rows, 1).reshape(
            shared_heads, group_size, block_rows
        )
        delta_block = lax.dynamic_slice_in_dim(delta_rows, start, block_rows, 1).reshape(
            shared_heads, group_size, block_rows
        )
        allowed = mask_rows(start, block_rows)
        allowed_wide = jnp.broadcast_to(
            allowed[:, None, :], (block_rows, group_size, key_count)
        ).reshape(block_rows * group_size, key_count)
        query_flat = query_block[:, 0].reshape(block_rows * group_size, head_size)
        out_flat = out_block[:, 0].reshape(block_rows * group_size, head_size)
        lse_flat = jnp.transpose(lse_block[0]).reshape(-1)
        delta_flat = jnp.transpose(delta_block[0]).reshape(-1)
        scores = (
            lax.dot_general(query_flat, key_list[0], contract, preferred_element_type=jnp.float32)
            * scaling
        )
        weights = jnp.where(allowed_wide, jnp.exp(scores - lse_flat[:, None]), jnp.float32(0.0))
        weights_low = weights.astype(jnp.bfloat16)
        weight_grads = lax.dot_general(
            out_flat, value_list[0], contract, preferred_element_type=jnp.float32
        )
        score_grads = (weights * (weight_grads - delta_flat[:, None])).astype(jnp.bfloat16)
        grad_query = jnp.dot(score_grads, key_list[0], preferred_element_type=jnp.float32) * scaling
        query_parts = [grad_query.reshape(block_rows, group_size, head_size)]
        new_keys = [
            lax.dot_general(score_grads, query_flat, across, preferred_element_type=jnp.float32)
            * scaling
        ]
        new_values = [
            lax.dot_general(weights_low, out_flat, across, preferred_element_type=jnp.float32)
        ]
        key_totals = key_totals + jnp.stack(new_keys, axis=1)
        value_totals = value_totals + jnp.stack(new_values, axis=1)
        grad_block = jnp.stack(query_parts, axis=1).reshape(block_rows, head_local, head_size)
        return ((key_totals, value_totals), grad_block)

    empty_grads = jnp.zeros(key_heads.shape, jnp.float32)
    totals, query_grads = lax.scan(
        block_step, (empty_grads, empty_grads), jnp.arange(block_count, dtype=jnp.int32)
    )
    return (query_grads.reshape(tok_count, head_local, head_size), totals[0], totals[1])


def local(
    grad_out,
    out_weight,
    queries,
    attn_out,
    lse,
    keys,
    values,
    prefix_keys,
    prefix_values,
    fork_owner,
    fork_root,
    fork_offset,
):
    tok_rows = queries.shape[0]
    head_local = lse.shape[0]
    shared_heads = keys.shape[1] // HD
    shared_width = keys.shape[1]
    servers_count = lax.axis_size("servers")
    my_index = lax.axis_index("servers")
    root_rows = ROOTS_DEV * RLEN
    out_grad = jnp.dot(grad_out, out_weight, preferred_element_type=jnp.float32).astype(
        jnp.bfloat16
    )
    out_heads = out_grad.reshape(tok_rows, head_local, HD)
    query_heads = queries.reshape(tok_rows, head_local, HD)
    output_heads = attn_out.reshape(tok_rows, head_local, HD)
    delta_rows = jnp.transpose(
        jnp.sum(out_heads.astype(jnp.float32) * output_heads.astype(jnp.float32), axis=2)
    )
    key_heads = keys.reshape(tok_rows, shared_heads, HD)
    value_heads = values.reshape(tok_rows, shared_heads, HD)
    gathered = (
        lax.all_gather(prefix_keys, "servers", axis=0, tiled=True),
        lax.all_gather(prefix_values, "servers", axis=0, tiled=True),
    )
    prompt_keys = gathered[0].reshape(-1, shared_heads, HD)
    prompt_values = gathered[1].reshape(-1, shared_heads, HD)
    prompt_count = prompt_keys.shape[0]

    def open_rows(start, rows):
        return jnp.ones((rows, prompt_count), dtype=jnp.bool_)

    pre_query_grad, pre_key_grad, pre_value_grad = attend(
        query_heads, out_heads, lse, delta_rows, prompt_keys, prompt_values, open_rows
    )
    prompt_sums = (
        lax.psum_scatter(
            pre_key_grad.reshape(-1, shared_width), "servers", scatter_dimension=0, tiled=True
        ),
        lax.psum_scatter(
            pre_value_grad.reshape(-1, shared_width), "servers", scatter_dimension=0, tiled=True
        ),
    )
    local_index = jnp.arange(tok_rows, dtype=jnp.int32)
    child_part = local_index - root_rows
    in_root = local_index < root_rows
    segment_ids = jnp.where(in_root, local_index // RLEN, ROOTS_DEV + child_part // CLEN)
    segment_pos = jnp.where(in_root, local_index % RLEN, child_part % CLEN)

    def own_rows(start, rows):
        query_seg = lax.dynamic_slice_in_dim(segment_ids, start, rows, 0)
        query_pos = lax.dynamic_slice_in_dim(segment_pos, start, rows, 0)
        return (query_seg[:, None] == segment_ids[None, :]) & (
            segment_pos[None, :] <= query_pos[:, None]
        )

    local_query_grad, local_key_grad, local_value_grad = attend(
        query_heads, out_heads, lse, delta_rows, key_heads, value_heads, own_rows
    )
    child_query = query_heads[root_rows:]
    child_out = out_heads[root_rows:]
    child_lse = lse[:, root_rows:]
    child_delta = delta_rows[:, root_rows:]
    owners_all = fork_owner[:, 0].reshape(servers_count, CH_DEV)
    roots_all = fork_root.reshape(servers_count, CH_DEV)
    my_owners = lax.dynamic_index_in_dim(owners_all, my_index, 0, keepdims=False)
    my_roots = lax.dynamic_index_in_dim(roots_all, my_index, 0, keepdims=False)
    my_offsets = lax.dynamic_slice_in_dim(fork_offset, my_index * CH_DEV, CH_DEV, 0)
    positions = jnp.arange(RLEN, dtype=jnp.int32)
    parent_key_index = jnp.arange(CH_DEV * RLEN, dtype=jnp.int32)
    parent_slot = parent_key_index // RLEN
    parent_pos = parent_key_index % RLEN

    def parent_rows(start, rows):
        child_ids = (start + jnp.arange(rows, dtype=jnp.int32)) // CLEN
        child_limit = jnp.take(my_offsets, child_ids, axis=0)
        return (child_ids[:, None] == parent_slot[None, :]) & (
            parent_pos[None, :] < child_limit[:, None]
        )

    root_keys = keys[:root_rows]
    root_values = values[:root_rows]
    all_roots = (
        lax.all_gather(root_keys, "servers", axis=0, tiled=True),
        lax.all_gather(root_values, "servers", axis=0, tiled=True),
    )
    parent_index = ((my_owners * ROOTS_DEV + my_roots) * RLEN)[:, None] + positions[None, :]
    flat_index = parent_index.reshape(-1)
    parent_keys = jnp.take(all_roots[0], flat_index, axis=0).reshape(
        CH_DEV * RLEN, shared_heads, HD
    )
    parent_values = jnp.take(all_roots[1], flat_index, axis=0).reshape(
        CH_DEV * RLEN, shared_heads, HD
    )
    parent_query_grad, parent_key_grad, parent_value_grad = attend(
        child_query, child_out, child_lse, child_delta, parent_keys, parent_values, parent_rows
    )
    dense_keys = (
        jnp.zeros((all_roots[0].shape[0], shared_width), jnp.float32)
        .at[flat_index]
        .add(parent_key_grad.reshape(-1, shared_width))
    )
    dense_values = (
        jnp.zeros((all_roots[1].shape[0], shared_width), jnp.float32)
        .at[flat_index]
        .add(parent_value_grad.reshape(-1, shared_width))
    )
    root_sums = (
        lax.psum_scatter(dense_keys, "servers", scatter_dimension=0, tiled=True),
        lax.psum_scatter(dense_values, "servers", scatter_dimension=0, tiled=True),
    )
    root_key_part = root_sums[0]
    root_value_part = root_sums[1]
    own_query_grad = pre_query_grad + local_query_grad
    grad_query = jnp.concatenate(
        [own_query_grad[:root_rows], own_query_grad[root_rows:] + parent_query_grad], axis=0
    )
    grad_queries = grad_query.astype(jnp.bfloat16).reshape(tok_rows, head_local * HD)
    local_keys = local_key_grad.reshape(tok_rows, shared_width)
    local_values = local_value_grad.reshape(tok_rows, shared_width)
    grad_keys = jnp.concatenate(
        [local_keys[:root_rows] + root_key_part, local_keys[root_rows:]], axis=0
    ).astype(jnp.bfloat16)
    grad_values = jnp.concatenate(
        [local_values[:root_rows] + root_value_part, local_values[root_rows:]], axis=0
    ).astype(jnp.bfloat16)
    prefix_grad_keys = prompt_sums[0].astype(jnp.bfloat16)
    prefix_grad_values = prompt_sums[1].astype(jnp.bfloat16)
    return (grad_queries, grad_keys, grad_values, prefix_grad_keys, prefix_grad_values)


def solution(mesh):
    placed = (
        P(("groups", "servers"), None),
        P(None, "heads"),
        P(("groups", "servers"), "heads"),
        P(("groups", "servers"), "heads"),
        P("heads", ("groups", "servers")),
        P(("groups", "servers"), "heads"),
        P(("groups", "servers"), "heads"),
        P(("groups", "servers"), "heads"),
        P(("groups", "servers"), "heads"),
        P("groups", None),
        P("groups"),
        P("groups"),
    )
    return jax.shard_map(
        local,
        mesh=mesh,
        in_specs=placed,
        out_specs=(
            P(("groups", "servers"), "heads"),
            P(("groups", "servers"), "heads"),
            P(("groups", "servers"), "heads"),
            P(("groups", "servers"), "heads"),
            P(("groups", "servers"), "heads"),
        ),
        check_vma=False,
    )
```

profile of v0, /device:TPU:0, one launch (start us, length us, event | category | flops | bytes accessed | tf_op | source)
XLA Modules:
  0.0 282.1 jit_solution(4056299993716482109)
XLA Ops:
  8.8 4.5 %convolution_convert_fusion = bf16[512,1024]{1,0:T(8,128)(2,1)S(1)} fusion(bf16[512,2048]{1,0:T(8,128)(2,1)S(1)} %copy-done, bf16[2048,1024]{1,0:T(8,128)(2,1)} %param.21), kind=kOutput, calls=%fused_computation.132 | convolution fusion | flops 2148007936 | bytes 7340032 | tf_op jit(solution)/shard_map/dot_general | solution.py:101
  20.3 14.8 %all_gather.12 = bf16[128,128]{1,0:T(8,128)(2,1)S(1)} all-gather(bf16[32,128]{1,0:T(8,128)(2,1)S(1)} %copy-done.16), channel_id=1, replica_groups=mesh['groups'=2,'servers'=4,'heads'=4] {'servers'}, dimensions={0}, use_global_device_ids=true | all-gather | bytes 40960 | tf_op jit(solution)/shard_map/all_gather | solution.py:113
  35.1 13.1 %all_gather.13 = bf16[128,128]{1,0:T(8,128)(2,1)S(1)} all-gather(bf16[32,128]{1,0:T(8,128)(2,1)S(1)} %copy-done.17), channel_id=1, replica_groups=mesh['groups'=2,'servers'=4,'heads'=4] {'servers'}, dimensions={0}, use_global_device_ids=true | all-gather | bytes 40960 | tf_op jit(solution)/shard_map/all_gather | solution.py:114
  52.2 34.4 %while.48 = (s32[]{:T(128)}, f32[128,1,128]{2,0,1:T(8,128)}, f32[128,1,128]{2,0,1:T(8,128)}, f32[4,128,8,128]{3,2,1,0:T(8,128)}, s32[4]{0:T(128)S(1)}, /*index=5...) while((s32[]{:T(128)}, f32[128,1,128]{2,0,1:T(8,128)}, ...), condition=%wide.region_2.3_spmd.clone, body=%wide.region_1.2_spmd.clone.sunk | while | flops 168771584 | bytes 4334310 | solution.py:74
  94.1 14.2 %all_gather.14 = bf16[1024,128]{1,0:T(8,128)(2,1)S(1)} all-gather(bf16[256,128]{1,0:T(8,128)(2,1)S(1)} %slice-done.1), channel_id=1, replica_groups=mesh['groups'=2,'servers'=4,'heads'=4] {'servers'}, dimensions={0}, use_global_device_ids=true | all-gather | bytes 327680 | tf_op jit(solution)/shard_map/all_gather | solution.py:174
  108.3 14.1 %all_gather.15 = bf16[1024,128]{1,0:T(8,128)(2,1)S(1)} all-gather(bf16[256,128]{1,0:T(8,128)(2,1)S(1)} %slice-done), channel_id=1, replica_groups=mesh['groups'=2,'servers'=4,'heads'=4] {'servers'}, dimensions={0}, use_global_device_ids=true | all-gather | bytes 327680 | tf_op jit(solution)/shard_map/all_gather | solution.py:175
  122.3 4.3 %gather_fusion = bf16[1024,128]{1,0:T(8,128)(2,1)} fusion(bf16[1024,128]{1,0:T(8,128)(2,1)S(1)} %all_gather.14, s32[1024]{0:T(1024)S(1)} %fusion.100), kind=kCustom, calls=%fused_computation.clone | custom fusion | bytes 528384 | tf_op jit(solution)/shard_map/jit(_take)/gather | solution.py:179
  126.6 4.3 %gather_fusion.1 = bf16[1024,128]{1,0:T(8,128)(2,1)} fusion(bf16[1024,128]{1,0:T(8,128)(2,1)S(1)} %all_gather.15, s32[1024]{0:T(1024)S(1)} %fusion.100), kind=kCustom, calls=%fused_computation.1.clone | custom fusion | bytes 528384 | tf_op jit(solution)/shard_map/jit(_take)/gather | solution.py:182
  136.1 56.4 %while.49 = (s32[]{:T(128)}, f32[1024,1,128]{2,0,1:T(8,128)S(1)}, f32[1024,1,128]{2,0,1:T(8,128)}, f32[2,128,8,128]{3,2,1,0:T(8,128)}, s32[2]{0:T(128)S(1)}, /*i...) while((s32[]{:T(128)}, f32[1024,1,128]{2,0,1:T(8,128)S(1)}, ...), condition=%wide.region_6.8_spmd.clone, body=%wide.region_5.7_spmd.clone.sunk | while | flops 1353864192 | bytes 51641432 | solution.py:74
  138.0 10.0 %and_select_fusion.4 = (s32[128]{0:T(128)S(1)}, s32[128]{0:T(128)S(1)}) fusion(s32[]{:T(128)} %bitcast.344, s32[]{:T(128)} %bitcast.345, s32[]{:T(128)} %bitcast.346, s32[]{:T(128)} %bitcast.347, s32[]{:T(128)} %bitcast.348, s32[]{:T(128)} %bitcast.349, s32[]{:T(128)} %bitcast.350, s32[]{:T(128)} %bitcast.351, s32[]{:T(128)} %bitcast.352, ...), kind=kLoop, calls=%fused_computation.89.clone.1 | loop fusion | flops 9216 | bytes 1092 | tf_op jit(solution)/shard_map/while/body/eval_jaxpr/jit(_take)/select_n | solution.py:166
  151.8 3.9 %multiply_convert_fusion.4 = bf16[1024,1024]{1,0:T(8,128)(2,1)S(1)} fusion(f32[1024,1024]{1,0:T(8,128)} %fusion.196, bf16[1024,128]{1,0:T(8,128)(2,1)} %get-tuple-element.918, f32[1024]{0:T(1024)S(1)} %sub.266, f32[1024]{0:T(1024)S(1)} %sub.267, pred[128,1024]{1,0:T(8,128)(4,1)} %compare_and_fusion.5, bf16[256,8,128]{2,1,0:T(8,128)(2,1)} %get-tuple-element.917, ...), kind=kOutput, calls=%fused_computation.35.clone.1 | convolution fusion | flops 274726912 | bytes 6955012 | tf_op jit(solution)/shard_map/while/body/eval_jaxpr/dot_general | solution.py:55
  165.7 10.0 %and_select_fusion.4 = (s32[128]{0:T(128)S(1)}, s32[128]{0:T(128)S(1)}) fusion(s32[]{:T(128)} %bitcast.344, s32[]{:T(128)} %bitcast.345, s32[]{:T(128)} %bitcast.346, s32[]{:T(128)} %bitcast.347, s32[]{:T(128)} %bitcast.348, s32[]{:T(128)} %bitcast.349, s32[]{:T(128)} %bitcast.350, s32[]{:T(128)} %bitcast.351, s32[]{:T(128)} %bitcast.352, ...), kind=kLoop, calls=%fused_computation.89.clone.1 | loop fusion | flops 9216 | bytes 1092 | tf_op jit(solution)/shard_map/while/body/eval_jaxpr/jit(_take)/select_n | solution.py:166
  179.5 3.9 %multiply_convert_fusion.4 = bf16[1024,1024]{1,0:T(8,128)(2,1)S(1)} fusion(f32[1024,1024]{1,0:T(8,128)} %fusion.196, bf16[1024,128]{1,0:T(8,128)(2,1)} %get-tuple-element.918, f32[1024]{0:T(1024)S(1)} %sub.266, f32[1024]{0:T(1024)S(1)} %sub.267, pred[128,1024]{1,0:T(8,128)(4,1)} %compare_and_fusion.5, bf16[256,8,128]{2,1,0:T(8,128)(2,1)} %get-tuple-element.917, ...), kind=kOutput, calls=%fused_computation.35.clone.1 | convolution fusion | flops 274726912 | bytes 6955012 | tf_op jit(solution)/shard_map/while/body/eval_jaxpr/dot_general | solution.py:55
  189.2 3.3 %fusion.200 = f32[1024,1,128]{2,0,1:T(8,128)} fusion(f32[1024,1024]{1,0:T(8,128)S(1)} %copy-done.2, f32[1024]{0:T(1024)S(1)} %sub.267, pred[128,1024]{1,0:T(8,128)(4,1)S(1)} %copy-done.9, f32[1024,1,128]{2,0,1:T(8,128)} %get-tuple-element.894, pred[]{:T(512)S(6)} %compare.245, bf16[256,8,128]{2,1,0:T(8,128)(2,1)S(1)} %copy-done.14, s32[]{:T(128)S(6)} %select_n.283), kind=kOutput, calls=%fused_computation.46.clone.1 | convolution fusion | flops 272891904 | bytes 5640197 | tf_op jit(solution)/shard_map/while/body/eval_jaxpr/dot_general | solution.py:66
  192.5 6.7 %scatter_custom_fusion.1 = f32[1024,128]{1,0:T(8,128)} fusion(s32[1024]{0:T(1024)S(1)} %bitcast.386, f32[1024,1,128]{2,0,1:T(8,128)} %get-tuple-element.322, f32[]{:T(128)} %constant.217.clone.1), kind=kCustom, calls=%fused_computation.140 | custom fusion | flops 131072 | bytes 1048580 | tf_op jit(solution)/shard_map/scatter-add | solution.py:196
  199.3 6.8 %scatter_custom_fusion = f32[1024,128]{1,0:T(8,128)} fusion(s32[1024]{0:T(1024)S(1)} %bitcast.387, f32[1024,1,128]{2,0,1:T(8,128)S(1)} %get-tuple-element.320, f32[]{:T(128)} %constant.217.clone.1), kind=kCustom, calls=%fused_computation.142 | custom fusion | flops 131072 | bytes 1048580 | tf_op jit(solution)/shard_map/scatter-add | solution.py:191
  207.6 56.9 %while.50 = (s32[]{:T(128)}, f32[512,1,128]{2,0,1:T(8,128)S(1)}, f32[512,1,128]{2,0,1:T(8,128)}, f32[4,128,8,128]{3,2,1,0:T(8,128)}, s32[4]{0:T(128)S(1)}, /*ind...) while((s32[]{:T(128)}, f32[512,1,128]{2,0,1:T(8,128)S(1)}, ...), condition=%wide.region_4.5_spmd.clone.clone, body=%wide.region_3.4_spmd.clone.clone.sunk | while | flops 675414016 | bytes 13156130 | solution.py:74
  210.1 3.0 %exponential_select_fusion.3 = f32[1024,512]{1,0:T(8,128)} fusion(bf16[512,128]{1,0:T(8,128)(2,1)S(1)} %get-tuple-element.1011, f32[1024]{0:T(1024)S(1)} %sub.272, pred[128,512]{1,0:T(8,128)(4,1)S(1)} %compare_and_fusion.6, bf16[512,8,128]{2,1,0:T(8,128)(2,1)} %get-tuple-element.1010, s32[]{:T(128)S(6)} %select_n.285), kind=kOutput, calls=%fused_computation.105.clone.1 | convolution fusion | flops 135790592 | bytes 2560004 | tf_op jit(solution)/shard_map/while/body/eval_jaxpr/dot_general | solution.py:50
  224.3 3.0 %exponential_select_fusion.3 = f32[1024,512]{1,0:T(8,128)} fusion(bf16[512,128]{1,0:T(8,128)(2,1)S(1)} %get-tuple-element.1011, f32[1024]{0:T(1024)S(1)} %sub.272, pred[128,512]{1,0:T(8,128)(4,1)S(1)} %compare_and_fusion.6, bf16[512,8,128]{2,1,0:T(8,128)(2,1)} %get-tuple-element.1010, s32[]{:T(128)S(6)} %select_n.285), kind=kOutput, calls=%fused_computation.105.clone.1 | convolution fusion | flops 135790592 | bytes 2560004 | tf_op jit(solution)/shard_map/while/body/eval_jaxpr/dot_general | solution.py:50
  233.2 2.9 %fusion.213 = f32[512,1,128]{2,0,1:T(8,128)} fusion(f32[1024,512]{1,0:T(8,128)} %exponential_select_fusion.3, f32[512,1,128]{2,0,1:T(8,128)} %get-tuple-element.988, bf16[512,8,128]{2,1,0:T(8,128)(2,1)} %get-tuple-element.1013, s32[]{:T(128)S(6)} %select_n.285, pred[]{:T(512)S(6)} %compare.246), kind=kOutput, calls=%fused_computation.112.clone.1 | convolution fusion | flops 134873088 | bytes 2883589 | tf_op jit(solution)/shard_map/while/body/eval_jaxpr/dot_general | solution.py:66
  238.6 3.0 %exponential_select_fusion.3 = f32[1024,512]{1,0:T(8,128)} fusion(bf16[512,128]{1,0:T(8,128)(2,1)S(1)} %get-tuple-element.1011, f32[1024]{0:T(1024)S(1)} %sub.272, pred[128,512]{1,0:T(8,128)(4,1)S(1)} %compare_and_fusion.6, bf16[512,8,128]{2,1,0:T(8,128)(2,1)} %get-tuple-element.1010, s32[]{:T(128)S(6)} %select_n.285), kind=kOutput, calls=%fused_computation.105.clone.1 | convolution fusion | flops 135790592 | bytes 2560004 | tf_op jit(solution)/shard_map/while/body/eval_jaxpr/dot_general | solution.py:50
  247.4 2.9 %fusion.213 = f32[512,1,128]{2,0,1:T(8,128)} fusion(f32[1024,512]{1,0:T(8,128)} %exponential_select_fusion.3, f32[512,1,128]{2,0,1:T(8,128)} %get-tuple-element.988, bf16[512,8,128]{2,1,0:T(8,128)(2,1)} %get-tuple-element.1013, s32[]{:T(128)S(6)} %select_n.285, pred[]{:T(512)S(6)} %compare.246), kind=kOutput, calls=%fused_computation.112.clone.1 | convolution fusion | flops 134873088 | bytes 2883589 | tf_op jit(solution)/shard_map/while/body/eval_jaxpr/dot_general | solution.py:66
  252.8 3.0 %exponential_select_fusion.3 = f32[1024,512]{1,0:T(8,128)} fusion(bf16[512,128]{1,0:T(8,128)(2,1)S(1)} %get-tuple-element.1011, f32[1024]{0:T(1024)S(1)} %sub.272, pred[128,512]{1,0:T(8,128)(4,1)S(1)} %compare_and_fusion.6, bf16[512,8,128]{2,1,0:T(8,128)(2,1)} %get-tuple-element.1010, s32[]{:T(128)S(6)} %select_n.285), kind=kOutput, calls=%fused_computation.105.clone.1 | convolution fusion | flops 135790592 | bytes 2560004 | tf_op jit(solution)/shard_map/while/body/eval_jaxpr/dot_general | solution.py:50
  261.7 2.9 %fusion.213 = f32[512,1,128]{2,0,1:T(8,128)} fusion(f32[1024,512]{1,0:T(8,128)} %exponential_select_fusion.3, f32[512,1,128]{2,0,1:T(8,128)} %get-tuple-element.988, bf16[512,8,128]{2,1,0:T(8,128)(2,1)} %get-tuple-element.1013, s32[]{:T(128)S(6)} %select_n.285, pred[]{:T(512)S(6)} %compare.246), kind=kOutput, calls=%fused_computation.112.clone.1 | convolution fusion | flops 134873088 | bytes 2883589 | tf_op jit(solution)/shard_map/while/body/eval_jaxpr/dot_general | solution.py:66
  (226 shorter events, 126.7 us)
Async XLA Ops:
  7.2 262.5 %reduce-scatter.9.cloned.1.call-start = ((), (), s32[]{:S(2)}) async-start(), calls=%async_computation.6 | async-start | bytes 81920 | tf_op jit(solution)/shard_map/reduce_scatter | solution.py:127
  17.7 17.4 %copy-start.17 = (bf16[32,128]{1,0:T(8,128)(2,1)S(1)}, bf16[32,128]{1,0:T(8,128)(2,1)}, u32[]{:S(2)}) copy-start(bf16[32,128]{1,0:T(8,128)(2,1)} %param.28) | copy-start | bytes 24580
  52.2 35.8 %copy-start.19 = (s32[64,1]{0,1:T(1,128)S(1)}, s32[64,1]{0,1:T(1,128)}, u32[]{:S(2)}) copy-start(s32[64,1]{0,1:T(1,128)} %param.29) | copy-start | bytes 772
  52.2 36.5 %copy-start.18 = (s32[64]{0:T(128)S(1)}, s32[64]{0:T(128)}, u32[]{:S(2)}) copy-start(s32[64]{0:T(128)} %param.30) | copy-start | bytes 772
  86.6 21.7 %copy-start.4 = (f32[8,512]{0,1:T(8,128)}, f32[8,512]{0,1:T(8,128)S(1)}, u32[]{:S(2)}) copy-start(f32[8,512]{0,1:T(8,128)S(1)} %get-tuple-element.1025) | copy-start | bytes 49156
  86.6 40.0 %copy-start.5 = (f32[8,512]{0,1:T(8,128)}, f32[8,512]{0,1:T(8,128)S(1)}, u32[]{:S(2)}) copy-start(f32[8,512]{0,1:T(8,128)S(1)} %get-tuple-element.1026) | copy-start | bytes 49156
  86.6 7.5 %slice-start.1 = ((bf16[512,128]{1,0:T(8,128)(2,1)}), bf16[256,128]{1,0:T(8,128)(2,1)S(1)}, s32[]{:S(2)}) async-start(bf16[512,128]{1,0:T(8,128)(2,1)} %param.25), calls=%async_computation.9 | async-start | bytes 131072 | tf_op jit(solution)/shard_map/slice | solution.py:171
  86.6 21.7 %slice-start = ((bf16[512,128]{1,0:T(8,128)(2,1)}), bf16[256,128]{1,0:T(8,128)(2,1)S(1)}, s32[]{:S(2)}) async-start(bf16[512,128]{1,0:T(8,128)(2,1)} %param.26), calls=%async_computation.8 | async-start | bytes 131072 | tf_op jit(solution)/shard_map/slice | solution.py:172
  86.6 184.4 %reduce-scatter.11.cloned.1.call-start = ((), (), s32[]{:S(2)}) async-start(), calls=%async_computation.7 | async-start | bytes 81920 | tf_op jit(solution)/shard_map/reduce_scatter | solution.py:130
  87.4 185.0 %reduce-scatter.7.cloned.1.call-start = ((), (), s32[]{:S(2)}) async-start(), calls=%async_computation.5 | async-start | bytes 655360 | tf_op jit(solution)/shard_map/reduce_scatter | solution.py:200
  126.6 7.4 %copy-start.20 = (s32[64]{0:T(128)S(1)}, s32[64]{0:T(128)}, u32[]{:S(2)}) copy-start(s32[64]{0:T(128)} %param.31) | copy-start | bytes 772
  158.5 2.8 copy-start.2
  158.5 2.8 copy-start.9
  158.5 3.0 %copy-start.14 = (bf16[256,8,128]{2,1,0:T(8,128)(2,1)S(1)}, bf16[256,8,128]{2,1,0:T(8,128)(2,1)}, u32[]{:S(2)}) copy-start(bf16[256,8,128]{2,1,0:T(8,128)(2,1)} %get-tuple-element.917) | copy-start | bytes 1572868 | tf_op jit(solution)/shard_map/while
  186.2 2.8 copy-start.2
  186.2 2.8 copy-start.9
  186.2 3.0 %copy-start.14 = (bf16[256,8,128]{2,1,0:T(8,128)(2,1)S(1)}, bf16[256,8,128]{2,1,0:T(8,128)(2,1)}, u32[]{:S(2)}) copy-start(bf16[256,8,128]{2,1,0:T(8,128)(2,1)} %get-tuple-element.917) | copy-start | bytes 1572868 | tf_op jit(solution)/shard_map/while
  199.2 8.4 %copy-start.6 = (bf16[512,128]{1,0:T(8,128)(2,1)S(1)}, bf16[512,128]{1,0:T(8,128)(2,1)}, u32[]{:S(2)}) copy-start(bf16[512,128]{1,0:T(8,128)(2,1)} %param.26) | copy-start | bytes 393220
  199.2 8.4 %copy-start.7 = (bf16[512,128]{1,0:T(8,128)(2,1)S(1)}, bf16[512,128]{1,0:T(8,128)(2,1)}, u32[]{:S(2)}) copy-start(bf16[512,128]{1,0:T(8,128)(2,1)} %param.25) | copy-start | bytes 393220
  199.2 74.7 %reduce-scatter.5.cloned.1.call-start = ((), (), s32[]{:S(2)}) async-start(), calls=%async_computation.4 | async-start | bytes 655360 | tf_op jit(solution)/shard_map/reduce_scatter | solution.py:199
  219.0 2.8 copy-start.8
  233.2 2.9 %copy-start.8 = (bf16[512,128]{1,0:T(8,128)(2,1)S(1)}, bf16[512,128]{1,0:T(8,128)(2,1)}, u32[]{:S(2)}) copy-start(bf16[512,128]{1,0:T(8,128)(2,1)} %get-tuple-element.1044) | copy-start | bytes 393220 | tf_op jit(solution)/shard_map/while
  247.4 2.9 %copy-start.8 = (bf16[512,128]{1,0:T(8,128)(2,1)S(1)}, bf16[512,128]{1,0:T(8,128)(2,1)}, u32[]{:S(2)}) copy-start(bf16[512,128]{1,0:T(8,128)(2,1)} %get-tuple-element.1044) | copy-start | bytes 393220 | tf_op jit(solution)/shard_map/while
  261.7 2.9 %copy-start.8 = (bf16[512,128]{1,0:T(8,128)(2,1)S(1)}, bf16[512,128]{1,0:T(8,128)(2,1)}, u32[]{:S(2)}) copy-start(bf16[512,128]{1,0:T(8,128)(2,1)} %get-tuple-element.1044) | copy-start | bytes 393220 | tf_op jit(solution)/shard_map/while
  (12 other events, 23.9 us)
Sparse Core Ops, SparseCore 0:
  86.8 20.0 reduce-scatter.8
  109.2 17.1 reduce-scatter.10
  199.3 23.3 reduce-scatter.6
  224.8 19.8 reduce-scatter.4
where the time goes:
time: 284 us; the launch traced here: 282 us
  matrix products  106 us (37%)
  blocking collectives  56.1 us (20%)
  other arithmetic  51.8 us (18%)
  local copies, waits for them, and re-layouts  45.9 us (16%)
  between operations  14 us (5%)
  loops' own time  6.92 us (2%)
    dot_general x10, matrix products, block_step(): lax.dot_general(weights_low, out_flat, across, preferred_element_type=jnp...  24.4 us
    dot_general x10, matrix products, block_step(): lax.dot_general(query_flat, key_list[0], contract, preferred_element_type...  22.1 us
    dot_general x10, matrix products, block_step(): lax.dot_general(out_flat, value_list[0], contract, preferred_element_type...  21.1 us
    select_n x2, other arithmetic, parent_rows(): child_limit = jnp.take(my_offsets, child_ids, axis=0)  20.1 us
    dot_general x10, matrix products, block_step(): lax.dot_general(score_grads, query_flat, across, preferred_element_type=j...  18.6 us
    unnamed x39, local copies, waits for them, and re-layouts  15.8 us
    dot_general x10, matrix products, block_step(): jnp.dot(score_grads, key_list[0], preferred_element_type=jnp.float32)  15.7 us
    all_gather x1, blocking collectives, local(): lax.all_gather(prefix_keys, 'servers', axis=0, tiled=True)  14.8 us
  transfers between devices with their start and end apart: 4, of which 0 were waited for; matrix products, arithmetic and copies ran while one was open for 53% of the time, Pallas kernels for 0%

commit v1 on v0

--- a/solution.py
+++ b/solution.py
@@ -9,6 +9,24 @@
 ROOTS_DEV = 4
 RLEN = 64
 CLEN = 16
+
+
+def ring_gather(value, axis, dim):
+    ways, here, hop = (lax.axis_size(axis), lax.axis_index(axis), value.shape[dim])
+    lengths = [n * ways if d == dim else n for d, n in enumerate(value.shape)]
+    full = lax.dynamic_update_slice_in_dim(
+        jnp.zeros(lengths, value.dtype), value, here * hop, axis=dim
+    )
+    going_up = going_down = value
+    for far in range(1, ways // 2 + 1):
+        going_up = lax.ppermute(going_up, axis, [(d, (d + 1) % ways) for d in range(ways)])
+        full = lax.dynamic_update_slice_in_dim(full, going_up, (here - far) % ways * hop, axis=dim)
+        if 2 * far < ways:
+            going_down = lax.ppermute(going_down, axis, [(d, (d - 1) % ways) for d in range(ways)])
+            full = lax.dynamic_update_slice_in_dim(
+                full, going_down, (here + far) % ways * hop, axis=dim
+            )
+    return full
 
 
 def attend(query_heads, out_heads, lse_rows, delta_rows, key_heads, value_heads, mask_rows):
@@ -171,7 +189,7 @@
     root_keys = keys[:root_rows]
     root_values = values[:root_rows]
     all_roots = (
-        lax.all_gather(root_keys, "servers", axis=0, tiled=True),
+        ring_gather(root_keys, "servers", 0),
         lax.all_gather(root_values, "servers", axis=0, tiled=True),
     )
     parent_index = ((my_owners * ROOTS_DEV + my_roots) * RLEN)[:, None] + positions[None, :]

time: 284 us -> 295 us (1.039)
  blocking collectives: 56.1 us -> 41.7 us
  waiting for transfers between devices: 0.77 us -> 11.5 us
  local copies, waits for them, and re-layouts: 45.9 us -> 54.9 us
  starting transfers between devices: 0.16 us -> 4.5 us
    all_gather x1 -> x0, blocking collectives: 14.2 us -> none  [local(): lax.all_gather(root_keys, 'servers', axis=0, tiled=True)]
    reduce_scatter x1, waiting for transfers between devices: 0.01 us -> 6.89 us  [local(): lax.psum_scatter(dense_keys, 'servers', scatter_dimension=0, tiled=True)]
    ppermute x0 -> x3, waiting for transfers between devices: none -> 4.52 us  [the longest x2 4.52 us: ring_gather(): lax.ppermute(going_up, axis, [(d, (d + 1) % ways) for d in range(ways)])]
    ppermute x0 -> x3, starting transfers between devices: none -> 4.11 us  [the longest x1 2.3 us: ring_gather(): lax.ppermute(going_down, axis, [(d, (d - 1) % ways) for d in range(ways)])]
    unnamed x39 -> x47, local copies, waits for them, and re-layouts: 15.8 us -> 17.7 us
  transfers between devices with their start and end apart: 4 -> 7, of which waited for: 0 -> 2; matrix products, arithmetic and copies ran while one was open for 53% -> 56% of each run, Pallas kernels for 0% -> 0%
where the time goes in v1:
time: 295 us; the launch traced here: 292 us
  matrix products  106 us (36%)
  local copies, waits for them, and re-layouts  54.9 us (19%)
  other arithmetic  52.8 us (18%)
  blocking collectives  41.7 us (14%)
  between operations  14.1 us (5%)
  waiting for transfers between devices  11.5 us (4%)
  loops' own time  7.07 us (2%)
  starting transfers between devices  4.5 us (2%)
    dot_general x10, matrix products, block_step(): lax.dot_general(weights_low, out_flat, across, preferred_element_type=jnp...  24.5 us
    dot_general x10, matrix products, block_step(): lax.dot_general(query_flat, key_list[0], contract, preferred_element_type...  24 us
    dot_general x10, matrix products, block_step(): lax.dot_general(out_flat, value_list[0], contract, preferred_element_type...  20.9 us
    select_n x2, other arithmetic, parent_rows(): child_limit = jnp.take(my_offsets, child_ids, axis=0)  19.9 us
    unnamed x47, local copies, waits for them, and re-layouts  17.7 us
    dot_general x10, matrix products, block_step(): lax.dot_general(score_grads, query_flat, across, preferred_element_type=j...  16.2 us
    dot_general x10, matrix products, block_step(): jnp.dot(score_grads, key_list[0], preferred_element_type=jnp.float32)  15.8 us
    all_gather x1, blocking collectives, local(): lax.all_gather(prefix_values, 'servers', axis=0, tiled=True)  14.8 us
  transfers between devices with their start and end apart: 7, of which 2 were waited for; matrix products, arithmetic and copies ran while one was open for 56% of the time, Pallas kernels for 0%

profile of v1, /device:TPU:0, one launch (start us, length us, event | category | flops | bytes accessed | tf_op | source)
XLA Modules:
  0.0 292.3 jit_solution(14036632177774455483)
XLA Ops:
  8.8 4.5 %convolution_convert_fusion = bf16[512,1024]{1,0:T(8,128)(2,1)S(1)} fusion(bf16[512,2048]{1,0:T(8,128)(2,1)S(1)} %copy-done, bf16[2048,1024]{1,0:T(8,128)(2,1)} %param.21), kind=kOutput, calls=%fused_computation.132 | convolution fusion | flops 2148007936 | bytes 7340032 | tf_op jit(solution)/shard_map/dot_general | solution.py:119
  19.1 14.8 %all_gather.10 = bf16[128,128]{1,0:T(8,128)(2,1)S(1)} all-gather(bf16[32,128]{1,0:T(8,128)(2,1)S(1)} %copy-done.19), channel_id=1, replica_groups=mesh['groups'=2,'servers'=4,'heads'=4] {'servers'}, dimensions={0}, use_global_device_ids=true | all-gather | bytes 40960 | tf_op jit(solution)/shard_map/all_gather | solution.py:132
  33.9 13.1 %all_gather.9 = bf16[128,128]{1,0:T(8,128)(2,1)S(1)} all-gather(bf16[32,128]{1,0:T(8,128)(2,1)S(1)} %copy-done.20), channel_id=1, replica_groups=mesh['groups'=2,'servers'=4,'heads'=4] {'servers'}, dimensions={0}, use_global_device_ids=true | all-gather | bytes 40960 | tf_op jit(solution)/shard_map/all_gather | solution.py:131
  51.0 31.9 %while.48 = (s32[]{:T(128)}, f32[128,1,128]{2,0,1:T(8,128)S(1)}, f32[128,1,128]{2,0,1:T(8,128)}, f32[4,128,8,128]{3,2,1,0:T(8,128)}, s32[4]{0:T(128)S(1)}, /*ind...) while((s32[]{:T(128)}, f32[128,1,128]{2,0,1:T(8,128)S(1)}, ...), condition=%wide.region_2.3_spmd.clone, body=%wide.region_1.2_spmd.clone.sunk | while | flops 168771584 | bytes 4334310 | solution.py:92
  96.8 13.8 %all_gather.11 = bf16[1024,128]{1,0:T(8,128)(2,1)S(1)} all-gather(bf16[256,128]{1,0:T(8,128)(2,1)S(1)} %slice-done), channel_id=1, replica_groups=mesh['groups'=2,'servers'=4,'heads'=4] {'servers'}, dimensions={0}, use_global_device_ids=true | all-gather | bytes 327680 | tf_op jit(solution)/shard_map/all_gather | solution.py:193
  115.1 3.2 %gather_fusion.1 = bf16[1024,128]{1,0:T(8,128)(2,1)S(1)} fusion(bf16[1024,128]{1,0:T(8,128)(2,1)S(1)} %all_gather.11, s32[1024]{0:T(1024)S(1)} %fusion.100), kind=kCustom, calls=%fused_computation.1.clone | custom fusion | bytes 528384 | tf_op jit(solution)/shard_map/jit(_take)/gather | solution.py:200
  120.4 4.5 %collective-permute-done.2 = bf16[256,128]{1,0:T(8,128)(2,1)S(1)} collective-permute-done((bf16[256,128]{1,0:T(8,128)(2,1)}, bf16[256,128]{1,0:T(8,128)(2,1)S(1)}, u32[]{:S(2)}, u32[]{:S(2)}) %collective-permute-start.2) | collective-permute-done | bytes 65568 | tf_op jit(solution)/shard_map/ppermute | solution.py:22
  125.0 4.3 %gather_fusion = bf16[1024,128]{1,0:T(8,128)(2,1)} fusion(bf16[1024,128]{1,0:T(8,128)(2,1)S(1)} %constant_dynamic-update-slice_fusion, s32[1024]{0:T(1024)S(1)} %fusion.100), kind=kCustom, calls=%fused_computation.clone | custom fusion | bytes 528384 | tf_op jit(solution)/shard_map/jit(_take)/gather | solution.py:197
  131.6 60.0 %while.49 = (s32[]{:T(128)}, f32[1024,1,128]{2,0,1:T(8,128)S(1)}, f32[1024,1,128]{2,0,1:T(8,128)}, f32[2,128,8,128]{3,2,1,0:T(8,128)}, s32[2]{0:T(128)}, /*index...) while((s32[]{:T(128)}, f32[1024,1,128]{2,0,1:T(8,128)S(1)}, ...), condition=%wide.region_6.8_spmd.clone, body=%wide.region_5.7_spmd.clone.sunk | while | flops 1353864192 | bytes 54197308 | solution.py:92
  134.3 10.0 %and_select_fusion.4 = (s32[128]{0:T(128)S(1)}, s32[128]{0:T(128)S(1)}) fusion(s32[]{:T(128)} %bitcast.344, s32[]{:T(128)} %bitcast.345, s32[]{:T(128)} %bitcast.346, s32[]{:T(128)} %bitcast.347, s32[]{:T(128)} %bitcast.348, s32[]{:T(128)} %bitcast.349, s32[]{:T(128)} %bitcast.350, s32[]{:T(128)} %bitcast.351, s32[]{:T(128)} %bitcast.352, ...), kind=kLoop, calls=%fused_computation.89.clone.1 | loop fusion | flops 9216 | bytes 1092 | tf_op jit(solution)/shard_map/while/body/eval_jaxpr/jit(_take)/select_n | solution.py:184
  144.4 3.7 %fusion.199 = f32[1024,1024]{1,0:T(8,128)} fusion(bf16[1024,128]{1,0:T(8,128)(2,1)S(1)} %get-tuple-element.917, bf16[256,8,128]{2,1,0:T(8,128)(2,1)} %get-tuple-element.916, s32[]{:T(128)S(6)} %select_n.316), kind=kOutput, calls=%fused_computation.52.clone.1 | convolution fusion | flops 268435456 | bytes 4718596 | tf_op jit(solution)/shard_map/while/body/eval_jaxpr/dot_general | solution.py:68
  149.2 3.8 %multiply_convert_fusion.4 = bf16[1024,1024]{1,0:T(8,128)(2,1)S(1)} fusion(f32[1024,1024]{1,0:T(8,128)} %fusion.199, bf16[1024,128]{1,0:T(8,128)(2,1)S(1)} %copy-done.17, f32[1024]{0:T(1024)S(1)} %sub.274, f32[1024]{0:T(1024)S(1)} %sub.275, pred[128,1024]{1,0:T(8,128)(4,1)S(1)} %compare_and_fusion.5, bf16[256,8,128]{2,1,0:T(8,128)(2,1)} %get-tuple-element.919, ...), kind=kOutput, calls=%fused_computation.35.clone.1 | convolution fusion | flops 274726912 | bytes 6955012 | tf_op jit(solution)/shard_map/while/body/eval_jaxpr/dot_general | solution.py:73
  163.7 10.0 %and_select_fusion.4 = (s32[128]{0:T(128)S(1)}, s32[128]{0:T(128)S(1)}) fusion(s32[]{:T(128)} %bitcast.344, s32[]{:T(128)} %bitcast.345, s32[]{:T(128)} %bitcast.346, s32[]{:T(128)} %bitcast.347, s32[]{:T(128)} %bitcast.348, s32[]{:T(128)} %bitcast.349, s32[]{:T(128)} %bitcast.350, s32[]{:T(128)} %bitcast.351, s32[]{:T(128)} %bitcast.352, ...), kind=kLoop, calls=%fused_computation.89.clone.1 | loop fusion | flops 9216 | bytes 1092 | tf_op jit(solution)/shard_map/while/body/eval_jaxpr/jit(_take)/select_n | solution.py:184
  173.9 3.7 %fusion.199 = f32[1024,1024]{1,0:T(8,128)} fusion(bf16[1024,128]{1,0:T(8,128)(2,1)S(1)} %get-tuple-element.917, bf16[256,8,128]{2,1,0:T(8,128)(2,1)} %get-tuple-element.916, s32[]{:T(128)S(6)} %select_n.316), kind=kOutput, calls=%fused_computation.52.clone.1 | convolution fusion | flops 268435456 | bytes 4718596 | tf_op jit(solution)/shard_map/while/body/eval_jaxpr/dot_general | solution.py:68
  178.6 3.8 %multiply_convert_fusion.4 = bf16[1024,1024]{1,0:T(8,128)(2,1)S(1)} fusion(f32[1024,1024]{1,0:T(8,128)} %fusion.199, bf16[1024,128]{1,0:T(8,128)(2,1)S(1)} %copy-done.17, f32[1024]{0:T(1024)S(1)} %sub.274, f32[1024]{0:T(1024)S(1)} %sub.275, pred[128,1024]{1,0:T(8,128)(4,1)S(1)} %compare_and_fusion.5, bf16[256,8,128]{2,1,0:T(8,128)(2,1)} %get-tuple-element.919, ...), kind=kOutput, calls=%fused_computation.35.clone.1 | convolution fusion | flops 274726912 | bytes 6955012 | tf_op jit(solution)/shard_map/while/body/eval_jaxpr/dot_general | solution.py:73
  188.3 3.3 %fusion.203 = f32[1024,1,128]{2,0,1:T(8,128)} fusion(f32[1024,1024]{1,0:T(8,128)S(1)} %copy-done.2, f32[1024]{0:T(1024)S(1)} %sub.275, pred[128,1024]{1,0:T(8,128)(4,1)S(1)} %compare_and_fusion.5, f32[1024,1,128]{2,0,1:T(8,128)} %get-tuple-element.896, pred[]{:T(512)S(6)} %compare.248, bf16[256,8,128]{2,1,0:T(8,128)(2,1)S(1)} %copy-done.16, ...), kind=kOutput, calls=%fused_computation.46.clone.1 | convolution fusion | flops 272891904 | bytes 5640197 | tf_op jit(solution)/shard_map/while/body/eval_jaxpr/dot_general | solution.py:84
  191.6 6.9 %scatter_custom_fusion.1 = f32[1024,128]{1,0:T(8,128)} fusion(s32[1024]{0:T(1024)} %bitcast.388, f32[1024,1,128]{2,0,1:T(8,128)} %get-tuple-element.322, f32[]{:T(128)} %constant.242.clone.1), kind=kCustom, calls=%fused_computation.140 | custom fusion | flops 131072 | bytes 1049088 | tf_op jit(solution)/shard_map/scatter-add | solution.py:214
  200.4 57.1 %while.50 = (s32[]{:T(128)}, f32[512,1,128]{2,0,1:T(8,128)S(1)}, f32[512,1,128]{2,0,1:T(8,128)}, f32[4,128,8,128]{3,2,1,0:T(8,128)}, s32[4]{0:T(128)S(1)}, /*ind...) while((s32[]{:T(128)}, f32[512,1,128]{2,0,1:T(8,128)S(1)}, ...), condition=%wide.region_4.5_spmd.clone.clone, body=%wide.region_3.4_spmd.clone.clone.sunk | while | flops 675414016 | bytes 13156314 | solution.py:92
  202.9 2.9 %exponential_select_fusion.3 = f32[1024,512]{1,0:T(8,128)} fusion(bf16[512,128]{1,0:T(8,128)(2,1)S(1)} %get-tuple-element.1013, f32[1024]{0:T(1024)S(1)} %sub.280, pred[128,512]{1,0:T(8,128)(4,1)S(1)} %compare_and_fusion.6, bf16[512,8,128]{2,1,0:T(8,128)(2,1)} %get-tuple-element.1012, s32[]{:T(128)S(6)} %select_n.318), kind=kOutput, calls=%fused_computation.105.clone.1 | convolution fusion | flops 135790592 | bytes 2560004 | tf_op jit(solution)/shard_map/while/body/eval_jaxpr/dot_general | solution.py:68
  217.1 3.0 %exponential_select_fusion.3 = f32[1024,512]{1,0:T(8,128)} fusion(bf16[512,128]{1,0:T(8,128)(2,1)S(1)} %get-tuple-element.1013, f32[1024]{0:T(1024)S(1)} %sub.280, pred[128,512]{1,0:T(8,128)(4,1)S(1)} %compare_and_fusion.6, bf16[512,8,128]{2,1,0:T(8,128)(2,1)} %get-tuple-element.1012, s32[]{:T(128)S(6)} %select_n.318), kind=kOutput, calls=%fused_computation.105.clone.1 | convolution fusion | flops 135790592 | bytes 2560004 | tf_op jit(solution)/shard_map/while/body/eval_jaxpr/dot_general | solution.py:68
  231.4 2.9 %exponential_select_fusion.3 = f32[1024,512]{1,0:T(8,128)} fusion(bf16[512,128]{1,0:T(8,128)(2,1)S(1)} %get-tuple-element.1013, f32[1024]{0:T(1024)S(1)} %sub.280, pred[128,512]{1,0:T(8,128)(4,1)S(1)} %compare_and_fusion.6, bf16[512,8,128]{2,1,0:T(8,128)(2,1)} %get-tuple-element.1012, s32[]{:T(128)S(6)} %select_n.318), kind=kOutput, calls=%fused_computation.105.clone.1 | convolution fusion | flops 135790592 | bytes 2560004 | tf_op jit(solution)/shard_map/while/body/eval_jaxpr/dot_general | solution.py:68
  245.7 2.9 %exponential_select_fusion.3 = f32[1024,512]{1,0:T(8,128)} fusion(bf16[512,128]{1,0:T(8,128)(2,1)S(1)} %get-tuple-element.1013, f32[1024]{0:T(1024)S(1)} %sub.280, pred[128,512]{1,0:T(8,128)(4,1)S(1)} %compare_and_fusion.6, bf16[512,8,128]{2,1,0:T(8,128)(2,1)} %get-tuple-element.1012, s32[]{:T(128)S(6)} %select_n.318), kind=kOutput, calls=%fused_computation.105.clone.1 | convolution fusion | flops 135790592 | bytes 2560004 | tf_op jit(solution)/shard_map/while/body/eval_jaxpr/dot_general | solution.py:68
  257.5 6.7 %scatter_custom_fusion = f32[1024,128]{1,0:T(8,128)} fusion(s32[1024]{0:T(1024)} %bitcast.389, f32[1024,1,128]{2,0,1:T(8,128)} %copy-done.3, f32[]{:T(128)} %constant.242.clone.1), kind=kCustom, calls=%fused_computation.142 | custom fusion | flops 131072 | bytes 1049088 | tf_op jit(solution)/shard_map/scatter-add | solution.py:209
  277.3 6.9 %reduce-scatter.5.cloned.1.call-done = f32[256,128]{1,0:T(8,128)} async-done(((f32[1024,128]{1,0:T(8,128)}), f32[256,128]{1,0:T(8,128)}) %reduce-scatter.5.cloned.1.call-update) | async-done | bytes 131088 | tf_op jit(solution)/shard_map/reduce_scatter | solution.py:217
  (254 shorter events, 142.4 us)
Async XLA Ops:
  7.2 263.6 %reduce-scatter.9.cloned.1.call-start = ((), (), s32[]{:S(2)}) async-start(), calls=%async_computation.6 | async-start | bytes 81920 | tf_op jit(solution)/shard_map/reduce_scatter | solution.py:145
  17.7 16.2 %copy-start.20 = (bf16[32,128]{1,0:T(8,128)(2,1)S(1)}, bf16[32,128]{1,0:T(8,128)(2,1)}, u32[]{:S(2)}) copy-start(bf16[32,128]{1,0:T(8,128)(2,1)} %param.27) | copy-start | bytes 24580
  51.0 38.1 %copy-start.22 = (s32[64,1]{0,1:T(1,128)S(1)}, s32[64,1]{0,1:T(1,128)}, u32[]{:S(2)}) copy-start(s32[64,1]{0,1:T(1,128)} %param.29) | copy-start | bytes 772
  51.0 38.9 %copy-start.21 = (s32[64]{0:T(128)S(1)}, s32[64]{0:T(128)}, u32[]{:S(2)}) copy-start(s32[64]{0:T(128)} %param.30) | copy-start | bytes 772
  83.0 29.6 %copy-start.7 = (f32[8,512]{0,1:T(8,128)}, f32[8,512]{0,1:T(8,128)S(1)}, u32[]{:S(2)}) copy-start(f32[8,512]{0,1:T(8,128)S(1)} %get-tuple-element.1027) | copy-start | bytes 49156
  83.0 13.8 %slice-start = ((bf16[512,128]{1,0:T(8,128)(2,1)}), bf16[256,128]{1,0:T(8,128)(2,1)S(1)}, s32[]{:S(2)}) async-start(bf16[512,128]{1,0:T(8,128)(2,1)} %param.26), calls=%async_computation.8 | async-start | bytes 131072 | tf_op jit(solution)/shard_map/slice | solution.py:190
  83.6 188.5 %reduce-scatter.11.cloned.1.call-start = ((), (), s32[]{:S(2)}) async-start(), calls=%async_computation.7 | async-start | bytes 81920 | tf_op jit(solution)/shard_map/reduce_scatter | solution.py:148
  84.6 33.8 %collective-permute-start = (bf16[256,128]{1,0:T(8,128)(2,1)S(1)}, bf16[256,128]{1,0:T(8,128)(2,1)}, u32[]{:S(2)}, u32[]{:S(2)}) collective-permute-start(bf16[256,128]{1,0:T(8,128)(2,1)S(1)} %get-tuple-element.601), channel_id=1, source_target_pairs={{0,4},{4,8},{8,12},{12,0},{1,5},{5,9},{9,13},{13,1},{2,6},{6,10},{... | collective-permute-start | bytes 196616 | tf_op jit(solution)/shard_map/ppermute | solution.py:22
  86.2 33.4 %collective-permute-start.1 = (bf16[256,128]{1,0:T(8,128)(2,1)S(1)}, bf16[256,128]{1,0:T(8,128)(2,1)}, u32[]{:S(2)}, u32[]{:S(2)}) collective-permute-start(bf16[256,128]{1,0:T(8,128)(2,1)S(1)} %get-tuple-element.601), channel_id=1, source_target_pairs={{0,12},{4,0},{8,4},{12,8},{1,13},{5,1},{9,5},{13,9},{2,14},{6,2},{... | collective-permute-start | bytes 196616 | tf_op jit(solution)/shard_map/ppermute | solution.py:25
  88.5 187.2 %reduce-scatter.7.cloned.1.call-start = ((), (), s32[]{:S(2)}) async-start(), calls=%async_computation.5 | async-start | bytes 655360 | tf_op jit(solution)/shard_map/reduce_scatter | solution.py:218
  110.6 7.7 %copy-start.23 = (s32[64]{0:T(128)S(1)}, s32[64]{0:T(128)}, u32[]{:S(2)}) copy-start(s32[64]{0:T(128)} %param.31) | copy-start | bytes 772
  118.5 6.5 %collective-permute-start.2 = (bf16[256,128]{1,0:T(8,128)(2,1)}, bf16[256,128]{1,0:T(8,128)(2,1)S(1)}, u32[]{:S(2)}, u32[]{:S(2)}) collective-permute-start(bf16[256,128]{1,0:T(8,128)(2,1)} %collective-permute-done), channel_id=1, source_target_pairs={{0,4},{4,8},{8,12},{12,0},{1,5},{5,9},{9,13},{13,1},{2,6},{6,10},{... | collective-permute-start | bytes 196616 | tf_op jit(solution)/shard_map/ppermute | solution.py:22
  144.4 4.8 %copy-start.17 = (bf16[1024,128]{1,0:T(8,128)(2,1)S(1)}, bf16[1024,128]{1,0:T(8,128)(2,1)}, u32[]{:S(2)}) copy-start(bf16[1024,128]{1,0:T(8,128)(2,1)} %get-tuple-element.920) | copy-start | bytes 786436 | tf_op jit(solution)/shard_map/while
  173.9 4.7 %copy-start.17 = (bf16[1024,128]{1,0:T(8,128)(2,1)S(1)}, bf16[1024,128]{1,0:T(8,128)(2,1)}, u32[]{:S(2)}) copy-start(bf16[1024,128]{1,0:T(8,128)(2,1)} %get-tuple-element.920) | copy-start | bytes 786436 | tf_op jit(solution)/shard_map/while
  191.6 8.8 %copy-start.3 = (f32[1024,1,128]{2,0,1:T(8,128)}, f32[1024,1,128]{2,0,1:T(8,128)S(1)}, u32[]{:S(2)}) copy-start(f32[1024,1,128]{2,0,1:T(8,128)S(1)} %get-tuple-element.320) | copy-start | bytes 1572868
  191.6 8.7 %copy-start.5 = (f32[512,1,128]{2,0,1:T(8,128)S(1)}, f32[512,1,128]{2,0,1:T(8,128)}, u32[]{:S(2)}) copy-start(f32[512,1,128]{2,0,1:T(8,128)} %custom-call.4) | copy-start | bytes 786436
  191.6 8.7 %copy-start.9 = (bf16[512,128]{1,0:T(8,128)(2,1)S(1)}, bf16[512,128]{1,0:T(8,128)(2,1)}, u32[]{:S(2)}) copy-start(bf16[512,128]{1,0:T(8,128)(2,1)} %param.26) | copy-start | bytes 393220
  191.6 8.7 %copy-start.10 = (bf16[512,128]{1,0:T(8,128)(2,1)S(1)}, bf16[512,128]{1,0:T(8,128)(2,1)}, u32[]{:S(2)}) copy-start(bf16[512,128]{1,0:T(8,128)(2,1)} %param.25) | copy-start | bytes 393220
  198.6 85.6 %reduce-scatter.5.cloned.1.call-start = ((), (), s32[]{:S(2)}) async-start(), calls=%async_computation.4 | async-start | bytes 655360 | tf_op jit(solution)/shard_map/reduce_scatter | solution.py:217
  210.2 4.4 %copy-start.25 = (s32[4]{0:T(128)S(1)}, s32[4]{0:T(128)}, u32[]{:S(2)}) copy-start(s32[4]{0:T(128)} %copy-done.24) | copy-start | bytes 52 | tf_op jit(solution)/shard_map/while
  224.5 4.4 %copy-start.25 = (s32[4]{0:T(128)S(1)}, s32[4]{0:T(128)}, u32[]{:S(2)}) copy-start(s32[4]{0:T(128)} %copy-done.24) | copy-start | bytes 52 | tf_op jit(solution)/shard_map/while
  238.8 4.4 %copy-start.25 = (s32[4]{0:T(128)S(1)}, s32[4]{0:T(128)}, u32[]{:S(2)}) copy-start(s32[4]{0:T(128)} %copy-done.24) | copy-start | bytes 52 | tf_op jit(solution)/shard_map/while
  253.0 4.4 %copy-start.25 = (s32[4]{0:T(128)S(1)}, s32[4]{0:T(128)}, u32[]{:S(2)}) copy-start(s32[4]{0:T(128)} %copy-done.24) | copy-start | bytes 52 | tf_op jit(solution)/shard_map/while
  269.9 5.8 %copy-start.6 = (f32[512,1,128]{2,0,1:T(8,128)S(1)}, f32[512,1,128]{2,0,1:T(8,128)}, u32[]{:S(2)}) copy-start(f32[512,1,128]{2,0,1:T(8,128)} %get-tuple-element.1031) | copy-start | bytes 786436
  (24 other events, 48.1 us)
Sparse Core Ops, SparseCore 0:
  83.7 20.0 reduce-scatter.8
  106.2 17.1 reduce-scatter.10
  198.7 19.9 reduce-scatter.6
  264.3 19.8 reduce-scatter.4
